TPU v7x, 32 devices: a whole 2x2x4 slice. The times are simulated.
32 devices in a mesh: pb: 4 (over y, core), wa: 8 (over z, x).
Axes of the slice: x: 2, y: 2, z: 4, core: 2. Of those that a mesh axis runs over, the one named last changes fastest.
Arguments:
- state: float32 [2, 8388608], P(None, ('pb', 'wa')), may hold values from -6 to 6
- gate_bank: float32 [4, 2, 128, 128], replicated, may hold values from -0.375 to 0.375
- pass_order: int32 [4], replicated, may hold values from 0 to 3, each once
Outputs:
- evolved: float32 [2, 8388608], P(None, ('pb', 'wa'))
Inputs may be any that keep to these rules, and one draw needn't show every extreme that they name: `pass_order`: each pass index 0 to 3 appears once.
All inputs are finite; a program needn't handle non-finite values.
Results may differ from a plain program's by a relative error of at most 0.0001.
Values sent between devices are 32-bit elements; how exact they have to be, the bound alone decides.
A program may use at most 64 MiB of HBM per device.

v0:
```python
import jax
import jax.numpy as jnp
from jax import lax
from jax.sharding import PartitionSpec as P

HIGH = lax.Precision.HIGHEST


def mix_left(gate, values):
    real = jnp.dot(gate[0], values[0], precision=HIGH) - jnp.dot(gate[1], values[1], precision=HIGH)
    imag = jnp.dot(gate[0], values[1], precision=HIGH) + jnp.dot(gate[1], values[0], precision=HIGH)
    return jnp.stack([real, imag])


def mix_right(gate, values):
    real = jnp.dot(values[0], gate[0].T, precision=HIGH) - jnp.dot(
        values[1], gate[1].T, precision=HIGH
    )
    imag = jnp.dot(values[1], gate[0].T, precision=HIGH) + jnp.dot(
        values[0], gate[1].T, precision=HIGH
    )
    return jnp.stack([real, imag])


def select_gate(gate_bank, pass_order, which):
    picked = pass_order[which] == jnp.arange(gate_bank.shape[0], dtype=jnp.int32)
    return jnp.sum(jnp.where(picked[:, None, None, None], gate_bank, 0.0), axis=0)


def trade_global(packed):
    return lax.all_to_all(
        lax.all_to_all(packed, "pb", split_axis=1, concat_axis=1, tiled=True),
        "wa",
        split_axis=2,
        concat_axis=2,
        tiled=True,
    )


def pack_block(block, groups, wa_count, middle):
    shaped = block.reshape(2, groups, 2, middle, wa_count // 2, -1)
    moved = jnp.transpose(shaped, (0, 1, 2, 4, 3, 5))
    return moved.reshape(2, groups, wa_count, middle, -1)


def unpack_block(packed, groups, wa_count, middle):
    shaped = packed.reshape(2, groups, 2, wa_count // 2, middle, -1)
    return jnp.transpose(shaped, (0, 1, 2, 4, 3, 5)).reshape(2, -1)


def per_device(state, gate_bank, pass_order):
    groups = lax.axis_size("pb")
    wa_count = lax.axis_size("wa")
    gate_rows = gate_bank.shape[2]
    middle = gate_rows // (2 * groups)
    psi = state
    first = select_gate(gate_bank, pass_order, 0)
    psi = mix_right(first, psi.reshape(2, -1, gate_rows)).reshape(2, -1)
    packed = trade_global(pack_block(psi, groups, wa_count, middle))
    second = select_gate(gate_bank, pass_order, 1)
    shaped = packed.reshape(2, groups, 2, wa_count // 2, middle, -1)
    moved = jnp.transpose(shaped, (0, 1, 2, 4, 3, 5))
    moved_shape = moved.shape
    mixed = mix_left(second, moved.reshape(2, gate_rows, -1)).reshape(moved_shape)
    psi = jnp.transpose(mixed, (0, 1, 2, 4, 3, 5)).reshape(2, -1)
    third = select_gate(gate_bank, pass_order, 2)
    psi = mix_right(third, psi.reshape(2, -1, gate_rows)).reshape(2, -1)
    fourth = select_gate(gate_bank, pass_order, 3)
    shaped = psi.reshape(2, groups, wa_count // 2, 2, middle, -1)
    moved = jnp.transpose(shaped, (0, 1, 3, 4, 2, 5))
    moved_shape = moved.shape
    mixed = mix_left(fourth, moved.reshape(2, gate_rows, -1)).reshape(moved_shape)
    packed = jnp.transpose(mixed, (0, 1, 4, 2, 3, 5)).reshape(2, groups, wa_count, middle, -1)
    psi = unpack_block(trade_global(packed), groups, wa_count, middle)
    return psi


def solution(mesh):
    in_specs = (P(None, ("pb", "wa")), P(), P())
    out_specs = P(None, ("pb", "wa"))
    return jax.shard_map(
        per_device, mesh=mesh, in_specs=in_specs, out_specs=out_specs, check_vma=False
    )
```

profile of v0, /device:TPU:0, one launch (start us, length us, event | category | flops | bytes accessed | tf_op | source)
XLA Modules:
  0.0 210.9 jit_solution(14688105302782742132)
XLA Ops:
  0.0 1.5 fusion.14
  1.5 4.3 %fusion.13 = (f32[1,262144]{1,0:T(1,128)S(1)}, f32[1,262144]{1,0:T(1,128)S(1)}) fusion(f32[2,262144]{1,0:T(2,128)} %param.3), kind=kLoop, calls=%fused_computation.42 | loop fusion | bytes 4194304 | tf_op jit(solution)/shard_map/slice | solution.py:16
  5.7 1.3 iota_compare_fusion
  7.0 1.2 iota_compare_fusion.2
  8.5 1.0 fusion.6
  9.5 1.0 fusion.7
  10.5 1.0 fusion
  11.6 1.0 fusion.1
  12.9 1.3 stack.36
  16.7 29.7 %all_to_all.20 = f32[2,4,8,16,512]{4,3,2,0,1:T(8,128)S(1)} all-to-all(f32[2,4,8,16,512]{4,3,2,0,1:T(8,128)S(1)} %bitcast.106), channel_id=1, replica_groups=mesh['pb'=4,'wa'=8] {'pb'}, dimensions={1} | all-to-all | bytes 4194304 | tf_op jit(solution)/shard_map/all_to_all | solution.py:32
  46.7 53.6 %all_to_all.21 = f32[2,4,8,16,512]{4,3,1,0,2:T(8,128)S(1)} all-to-all(f32[2,4,8,16,512]{4,3,1,0,2:T(8,128)S(1)} %copy.29), channel_id=1, replica_groups=mesh['pb'=4,'wa'=8] {'wa'}, dimensions={2} | all-to-all | bytes 4194304 | tf_op jit(solution)/shard_map/all_to_all | solution.py:31
  100.3 1.4 copy.48
  104.9 1.0 convolution_add_fusion.2
  105.9 1.0 convolution_subtract_fusion.2
  107.7 1.3 copy.31
  113.7 1.2 convolution_subtract_fusion.1
  119.4 1.0 fusion.3
  120.4 1.0 convolution_add_fusion
  121.5 1.0 convolution_subtract_fusion
  123.2 1.3 copy.35
  126.3 28.1 %all_to_all.22 = f32[2,4,8,16,512]{4,3,2,0,1:T(8,128)S(1)} all-to-all(f32[2,4,8,16,512]{4,3,2,0,1:T(8,128)S(1)} %copy.37), channel_id=1, replica_groups=mesh['pb'=4,'wa'=8] {'pb'}, dimensions={1} | all-to-all | bytes 4194304 | tf_op jit(solution)/shard_map/all_to_all | solution.py:32
  154.7 51.3 %all_to_all.23 = f32[2,4,8,16,512]{4,3,1,0,2:T(8,128)S(1)} all-to-all(f32[2,4,8,16,512]{4,3,1,0,2:T(8,128)S(1)} %copy.38), channel_id=1, replica_groups=mesh['pb'=4,'wa'=8] {'wa'}, dimensions={2} | all-to-all | bytes 4194304 | tf_op jit(solution)/shard_map/all_to_all | solution.py:31
  206.0 1.4 copy.40
  207.4 3.5 %reshape.72 = f32[2,262144]{1,0:T(2,128)} reshape(f32[2,4,2,16,4,512]{5,4,3,2,1,0:T(4,128)S(1)} %copy.40) | data formatting | bytes 4194304 | tf_op jit(solution)/shard_map/reshape | solution.py:48
  (45 shorter events, 19.0 us)
Async XLA Ops:
  1.5 6.8 %copy-start.3 = (f32[4,2,128,128]{3,2,1,0:T(8,128)S(1)}, f32[4,2,128,128]{3,2,1,0:T(8,128)}, u32[]{:S(2)}) copy-start(f32[4,2,128,128]{3,2,1,0:T(8,128)} %param.4) | copy-start | bytes 1572868
  14.3 1.2 copy-start
  108.9 1.2 copy-start.1
  124.5 1.2 copy-start.2
where the time goes:
time: 211 us
  blocking collectives  163 us (77%)
  local copies, waits for them, and re-layouts  27.2 us (13%)
  matrix products  16.4 us (8%)
  other arithmetic  4.25 us (2%)
    all_to_all x2, blocking collectives, trade_global(): lax.all_to_all(lax.all_to_all(packed, 'pb', split_axis=1, concat_axis=1,...  105 us
    all_to_all x2, blocking collectives, trade_global(): lax.all_to_all(packed, 'pb', split_axis=1, concat_axis=1, tiled=True)  57.9 us
    another operation x8, local copies, waits for them, and re-layouts, mix_left(): return jnp.stack([real, imag])  6.06 us
    slice x2, local copies, waits for them, and re-layouts, mix_right(): values[0]  4.46 us

commit v1 on v0

--- a/solution.py
+++ b/solution.py
@@ -28,12 +28,20 @@
 
 
 def trade_global(packed):
-    return lax.all_to_all(
-        lax.all_to_all(packed, "pb", split_axis=1, concat_axis=1, tiled=True),
-        "wa",
-        split_axis=2,
-        concat_axis=2,
-        tiled=True,
+    return jnp.concatenate(
+        lax.all_to_all(
+            jnp.stack(
+                jnp.split(
+                    lax.all_to_all(packed, "pb", split_axis=1, concat_axis=1, tiled=True),
+                    lax.axis_size("wa"),
+                    axis=2,
+                )
+            ),
+            "wa",
+            0,
+            0,
+        ),
+        axis=2,
     )
 
 

time: 211 us -> 211 us (level)
  no operation moved by 1% of the time
where the time goes in v1:
time: 211 us
  blocking collectives  163 us (77%)
  local copies, waits for them, and re-layouts  27.2 us (13%)
  matrix products  16.4 us (8%)
  other arithmetic  4.25 us (2%)
    all_to_all x2, blocking collectives, trade_global(): lax.all_to_all(jnp.stack(jnp.split(lax.all_to_all(packed, 'pb', split_axi...  105 us
    all_to_all x2, blocking collectives, trade_global(): lax.all_to_all(packed, 'pb', split_axis=1, concat_axis=1, tiled=True)  57.9 us
    another operation x8, local copies, waits for them, and re-layouts, mix_left(): return jnp.stack([real, imag])  6.06 us
    slice x2, local copies, waits for them, and re-layouts, mix_right(): values[0]  4.46 us

profile of v1, /device:TPU:0, one launch (start us, length us, event | category | flops | bytes accessed | tf_op | source)
XLA Modules:
  0.0 211.0 jit_solution(6162761487790879801)
XLA Ops:
  0.0 1.5 fusion.30
  1.5 4.3 %fusion.29 = (f32[1,262144]{1,0:T(1,128)S(1)}, f32[1,262144]{1,0:T(1,128)S(1)}) fusion(f32[2,262144]{1,0:T(2,128)} %param.3), kind=kLoop, calls=%fused_computation.74 | loop fusion | bytes 4194304 | tf_op jit(solution)/shard_map/slice | solution.py:16
  5.7 1.3 iota_compare_fusion
  7.0 1.2 iota_compare_fusion.2
  8.5 1.0 fusion.22
  9.5 1.0 fusion.23
  10.5 1.0 fusion
  11.6 1.0 fusion.1
  12.9 1.3 stack.90
  16.7 29.7 %all_to_all.20 = f32[2,4,8,16,512]{4,3,2,0,1:T(8,128)S(1)} all-to-all(f32[2,4,8,16,512]{4,3,2,0,1:T(8,128)S(1)} %bitcast.201), channel_id=1, replica_groups=mesh['pb'=4,'wa'=8] {'pb'}, dimensions={1} | all-to-all | bytes 4194304 | tf_op jit(solution)/shard_map/all_to_all | solution.py:35
  46.6 53.6 %all_to_all.21 = f32[8,2,4,1,16,512]{5,4,1,2,3,0:T(8,128)S(1)} all-to-all(f32[8,2,4,1,16,512]{5,4,1,2,3,0:T(8,128)S(1)} %fusion.10), channel_id=1, replica_groups=mesh['pb'=4,'wa'=8] {'wa'}, dimensions={0} | all-to-all | bytes 4194304 | tf_op jit(solution)/shard_map/all_to_all | solution.py:32
  100.2 1.4 copy.147
  102.8 1.0 fusion.20
  104.8 1.0 convolution_add_fusion.2
  105.8 1.0 convolution_subtract_fusion.2
  107.6 1.3 copy.109
  113.6 1.2 convolution_subtract_fusion.1
  120.3 1.0 convolution_add_fusion
  121.4 1.0 convolution_subtract_fusion
  123.1 1.3 copy.113
  126.2 28.1 %all_to_all.22 = f32[2,4,8,16,512]{4,3,2,0,1:T(8,128)S(1)} all-to-all(f32[2,4,8,16,512]{4,3,2,0,1:T(8,128)S(1)} %copy.115), channel_id=1, replica_groups=mesh['pb'=4,'wa'=8] {'pb'}, dimensions={1} | all-to-all | bytes 4194304 | tf_op jit(solution)/shard_map/all_to_all | solution.py:35
  154.8 51.3 %all_to_all.23 = f32[8,2,4,1,16,512]{5,4,2,1,3,0:T(8,128)S(1)} all-to-all(f32[8,2,4,1,16,512]{5,4,2,1,3,0:T(8,128)S(1)} %copy.123), channel_id=1, replica_groups=mesh['pb'=4,'wa'=8] {'wa'}, dimensions={0} | all-to-all | bytes 4194304 | tf_op jit(solution)/shard_map/all_to_all | solution.py:32
  206.1 1.4 copy.125
  207.5 3.5 %reshape.72 = f32[2,262144]{1,0:T(2,128)} reshape(f32[2,4,2,16,4,512]{5,4,3,2,1,0:T(4,128)S(1)} %copy.125) | data formatting | bytes 4194304 | tf_op jit(solution)/shard_map/reshape | solution.py:56
  (60 shorter events, 19.0 us)
Async XLA Ops:
  1.5 6.8 %copy-start.3 = (f32[4,2,128,128]{3,2,1,0:T(8,128)S(1)}, f32[4,2,128,128]{3,2,1,0:T(8,128)}, u32[]{:S(2)}) copy-start(f32[4,2,128,128]{3,2,1,0:T(8,128)} %param.4) | copy-start | bytes 1572868
  14.3 1.2 copy-start
  108.9 1.2 copy-start.1
  124.4 1.2 copy-start.2
